TPU v7x, 512 devices: a whole 4x4x16 slice. The times are simulated.
512 devices in a mesh: sec: 64 (over y, z), mpo: 8 (over x, core).
Axes of the slice: x: 4, y: 4, z: 16, core: 2. Of those that a mesh axis runs over, the one named last changes fastest.
Arguments:
- wavefunction: bfloat16 [64, 8, 512, 256], P('sec', None, 'mpo'), may hold values from -6 to 6
- left_env: bfloat16 [64, 40, 512, 512], P('sec', 'mpo'), may hold values from -0.0390625 to 0.0390625
- right_env: bfloat16 [64, 40, 256, 256], P('sec', 'mpo'), may hold values from -0.375 to 0.375
- left_dims: int32 [64], P('sec'), may hold values from 256 to 512
- right_dims: int32 [64], P('sec'), may hold values from 128 to 256
- term_shift: int32 [40], P('mpo'), may hold values from 0 to 4, as said below
Outputs:
- product: bfloat16 [64, 8, 512, 256], P('sec', None, 'mpo')
Inputs may be any that keep to these rules, and one draw needn't show every extreme that they name: `term_shift`: each of the five classes is named by exactly 8 terms.
All inputs are finite; a program needn't handle non-finite values.
Results may differ from a plain program's by a relative error of at most 0.0049.
Values may be sent and summed in bfloat16 or wider, within the bound.
A program may use at most 64 MiB of HBM per device.

v0:
```python
import jax
import jax.numpy as jnp
from jax import lax
from jax.sharding import PartitionSpec as P

SPINS = 8


number_steps = (0, 1, -1, 1, -1)
spin_steps = (0, 1, -1, -1, 1)


def shifted(array, axis, by):
    length = lax.axis_size(axis)
    pairs = [(i, i + by) for i in range(length) if 0 <= i + by < length]
    return lax.ppermute(array, axis, pairs)


def per_device(wavefunction, left_env, right_env, left_dims, right_dims, term_shift):
    row_share = wavefunction.shape[2]
    columns = wavefunction.shape[3]
    mpo_place = lax.axis_index("mpo")
    sector_id = lax.axis_index("sec")
    lattice_rows = lax.axis_size("sec") // SPINS
    rows_here = mpo_place * row_share + jnp.arange(row_share, dtype=jnp.int32)
    column_ids = jnp.arange(columns, dtype=jnp.int32)
    keep_mask = (rows_here[:, None] < left_dims[0]) & (column_ids[None, :] < right_dims[0])
    live_block = jnp.where(keep_mask[None, None], wavefunction, jnp.zeros_like(wavefunction))
    sector_line = sector_id // SPINS
    sector_place = sector_id % SPINS
    line_steps = jnp.array(number_steps, dtype=jnp.int32)
    place_steps = jnp.array(spin_steps, dtype=jnp.int32)
    source_line = sector_line - line_steps
    source_place = sector_place - place_steps
    inside = (
        (source_line >= 0)
        & (source_line < lattice_rows)
        & (source_place >= 0)
        & (source_place < SPINS)
    )
    selector = (
        (term_shift[:, None] == jnp.arange(5, dtype=jnp.int32)[None, :]) & inside[None, :]
    ).astype(jnp.bfloat16)
    full_block = lax.all_gather(live_block, "mpo", axis=2, tiled=True)
    neighbours = [full_block]
    for shift_class in range(1, 5):
        offset = number_steps[shift_class] * SPINS + spin_steps[shift_class]
        neighbours.append(shifted(full_block, "sec", offset))
    stacked = jnp.concatenate(neighbours, axis=0)
    selected = jnp.einsum(
        "tc,cvpq->tvpq", selector, stacked, preferred_element_type=jnp.float32
    ).astype(jnp.bfloat16)
    left_terms = left_env[0]
    right_terms = right_env[0]
    applied = jnp.einsum(
        "tpk,tvkq->tvpq", left_terms, selected, preferred_element_type=jnp.float32
    ).astype(jnp.bfloat16)
    term_total = jnp.einsum(
        "tvpk,tqk->vpq", applied, right_terms, preferred_element_type=jnp.float32
    )[None]
    row_sums = lax.psum_scatter(term_total, "mpo", scatter_dimension=2, tiled=True)
    return jnp.where(keep_mask[None, None], row_sums, jnp.zeros_like(row_sums)).astype(jnp.bfloat16)


def solution(mesh):
    in_specs = (
        P("sec", None, "mpo", None),
        P("sec", "mpo", None, None),
        P("sec", "mpo", None, None),
        P("sec"),
        P("sec"),
        P("mpo"),
    )
    out_specs = P("sec", None, "mpo", None)
    return jax.shard_map(
        per_device, mesh=mesh, in_specs=in_specs, out_specs=out_specs, check_vma=False
    )
```

profile of v0, /device:TPU:1, one launch (start us, length us, event | category | flops | bytes accessed | tf_op | source)
XLA Modules:
  0.0 791.8 jit_solution(16231609190747013689)
XLA Ops:
  6.5 0.0 copy-start
  6.5 0.0 all-gather.2.cloned.1.call-start
  8.0 0.1 broadcast_and_fusion
  8.1 1.7 broadcast_select_fusion
  9.8 0.0 all-gather.2.cloned.1.call-update
  9.8 0.0 reduce-scatter.2.cloned.1.call-start
  9.9 38.7 %all-gather.2.cloned.1.call-done = bf16[1,8,512,256]{3,2,1,0:T(8,128)(2,1)} async-done(((bf16[1,8,64,256]{3,2,1,0:T(8,128)(2,1)}), bf16[1,8,512,256]{3,2,1,0:T(8,128)(2,1)}) %all-gather.2.cloned.1.call-update) | async-done | bytes 2097168 | tf_op jit(solution)/shard_map/all_gather | solution.py:44
  48.6 13.1 %collective-permute-start = (bf16[1,8,512,256]{3,2,1,0:T(8,128)(2,1)}, bf16[1,8,512,256]{3,2,1,0:T(8,128)(2,1)}, u32[]{:S(2)}, u32[]{:S(2)}) collective-permute-start(bf16[1,8,512,256]{3,2,1,0:T(8,128)(2,1)} %all-gather.2.cloned.1.call-done), channel_id=1, source_target_pairs={{0,72},{8,80},{16,88},{24,96},{32,104},{40,112},{48,120},{56,128},... | collective-permute-start | bytes 6291464 | tf_op jit(solution)/shard_map/ppermute | solution.py:16
  61.6 1.3 collective-permute-start.1
  62.9 2.7 collective-permute-start.2
  65.6 1.3 collective-permute-start.3
  66.9 0.7 compare_and_fusion
  67.6 0.0 copy-start.1
  67.6 1.7 constant_dynamic-update-slice_fusion.4
  69.3 303.3 %collective-permute-done = bf16[1,8,512,256]{3,2,1,0:T(8,128)(2,1)} collective-permute-done((bf16[1,8,512,256]{3,2,1,0:T(8,128)(2,1)}, bf16[1,8,512,256]{3,2,1,0:T(8,128)(2,1)}, u32[]{:S(2)}, u32[]{:S(2)}) %collective-permute-start) | collective-permute-done | bytes 2097184 | tf_op jit(solution)/shard_map/ppermute | solution.py:16
  372.7 1.7 constant_dynamic-update-slice_fusion.3
  374.4 3.2 collective-permute-done.1
  377.6 1.7 constant_dynamic-update-slice_fusion.2
  379.3 0.0 collective-permute-done.2
  379.3 1.7 constant_dynamic-update-slice_fusion.1
  381.1 90.3 %collective-permute-done.3 = bf16[1,8,512,256]{3,2,1,0:T(8,128)(2,1)} collective-permute-done((bf16[1,8,512,256]{3,2,1,0:T(8,128)(2,1)}, bf16[1,8,512,256]{3,2,1,0:T(8,128)(2,1)}, u32[]{:S(2)}, u32[]{:S(2)}) %collective-permute-start.3) | collective-permute-done | bytes 2097184 | tf_op jit(solution)/shard_map/ppermute | solution.py:16
  471.4 1.7 constant_dynamic-update-slice_fusion
  473.1 0.0 copy-done.1
  473.1 0.0 copy-start.2
  473.1 24.2 %fusion = bf16[5,8,512,256]{3,0,2,1:T(8,128)(2,1)} fusion(bf16[5,8,512,256]{3,2,1,0:T(8,128)(2,1)S(1)} %constant_dynamic-update-slice_fusion, s32[5]{0:T(128)S(1)} %copy-done.1, pred[5]{0:T(512)(128)(4,1)S(1)} %compare_and_fusion), kind=kOutput, calls=%fused_computation.1 | convolution fusion | flops 52428848 | bytes 20971544 | tf_op jit(solution)/shard_map/tc,cvpq->tvpq/dot_general | solution.py:50
  497.3 0.0 copy-done
  497.3 0.0 copy-done.2
  497.3 16.6 %fusion.13 = f32[1,8,512,256]{3,2,1,0:T(8,128)} fusion(bf16[1,5,512,512]{3,2,1,0:T(8,128)(2,1)S(1)} %copy-done, bf16[1,5,256,256]{3,2,1,0:T(8,128)(2,1)S(1)} %copy-done.2, bf16[5,8,512,256]{3,0,2,1:T(8,128)(2,1)} %fusion), kind=kOutput, calls=%fused_computation.9 | convolution fusion | flops 8058306560 | bytes 17956864 | tf_op jit(solution)/shard_map/tvpk,tqk->vpq/dot_general | solution.py:58
  514.0 0.0 reduce-scatter.2.cloned.1.call-update
  514.0 269.2 %reduce-scatter.2.cloned.1.call-done = f32[1,8,64,256]{3,2,1,0:T(8,128)} async-done(((f32[1,8,512,256]{3,2,1,0:T(8,128)}), f32[1,8,64,256]{3,2,1,0:T(8,128)}) %reduce-scatter.2.cloned.1.call-update) | async-done | bytes 524304 | tf_op jit(solution)/shard_map/reduce_scatter | solution.py:61
  783.2 1.8 select_convert_fusion
  (2 shorter events, 0.0 us)
Async XLA Ops:
  6.5 490.8 %copy-start = (bf16[1,5,512,512]{3,2,1,0:T(8,128)(2,1)S(1)}, bf16[1,5,512,512]{3,2,1,0:T(8,128)(2,1)}, u32[]{:S(2)}) copy-start(bf16[1,5,512,512]{3,2,1,0:T(8,128)(2,1)} %param.9) | copy-start | bytes 7864324
  6.5 42.1 %all-gather.2.cloned.1.call-start = ((), (), s32[]{:S(2)}) async-start(), calls=%async_computation.1 | async-start | bytes 2359296 | tf_op jit(solution)/shard_map/all_gather | solution.py:44
  9.8 773.4 %reduce-scatter.2.cloned.1.call-start = ((), (), s32[]{:S(2)}) async-start(), calls=%async_computation.2 | async-start | bytes 4718592 | tf_op jit(solution)/shard_map/reduce_scatter | solution.py:61
  48.6 324.1 %collective-permute-start = (bf16[1,8,512,256]{3,2,1,0:T(8,128)(2,1)}, bf16[1,8,512,256]{3,2,1,0:T(8,128)(2,1)}, u32[]{:S(2)}, u32[]{:S(2)}) collective-permute-start(bf16[1,8,512,256]{3,2,1,0:T(8,128)(2,1)} %all-gather.2.cloned.1.call-done), channel_id=1, source_target_pairs={{0,72},{8,80},{16,88},{24,96},{32,104},{40,112},{48,120},{56,128},... | collective-permute-start | bytes 6291464 | tf_op jit(solution)/shard_map/ppermute | solution.py:16
  61.6 315.9 %collective-permute-start.1 = (bf16[1,8,512,256]{3,2,1,0:T(8,128)(2,1)}, bf16[1,8,512,256]{3,2,1,0:T(8,128)(2,1)}, u32[]{:S(2)}, u32[]{:S(2)}) collective-permute-start(bf16[1,8,512,256]{3,2,1,0:T(8,128)(2,1)} %all-gather.2.cloned.1.call-done), channel_id=1, source_target_pairs={{72,0},{80,8},{88,16},{96,24},{104,32},{112,40},{120,48},{128,56},... | collective-permute-start | bytes 6291464 | tf_op jit(solution)/shard_map/ppermute | solution.py:16
  62.9 316.4 %collective-permute-start.2 = (bf16[1,8,512,256]{3,2,1,0:T(8,128)(2,1)}, bf16[1,8,512,256]{3,2,1,0:T(8,128)(2,1)}, u32[]{:S(2)}, u32[]{:S(2)}) collective-permute-start(bf16[1,8,512,256]{3,2,1,0:T(8,128)(2,1)} %all-gather.2.cloned.1.call-done), channel_id=1, source_target_pairs={{0,56},{8,64},{16,72},{24,80},{32,88},{40,96},{48,104},{56,112},{6... | collective-permute-start | bytes 6291464 | tf_op jit(solution)/shard_map/ppermute | solution.py:16
  65.6 405.8 %collective-permute-start.3 = (bf16[1,8,512,256]{3,2,1,0:T(8,128)(2,1)}, bf16[1,8,512,256]{3,2,1,0:T(8,128)(2,1)}, u32[]{:S(2)}, u32[]{:S(2)}) collective-permute-start(bf16[1,8,512,256]{3,2,1,0:T(8,128)(2,1)} %all-gather.2.cloned.1.call-done), channel_id=1, source_target_pairs={{56,0},{64,8},{72,16},{80,24},{88,32},{96,40},{104,48},{112,56},{1... | collective-permute-start | bytes 6291464 | tf_op jit(solution)/shard_map/ppermute | solution.py:16
  67.6 405.5 %copy-start.1 = (s32[5]{0:T(128)S(1)}, s32[5]{0:T(128)}, u32[]{:S(2)}) copy-start(s32[5]{0:T(128)} %param.13) | copy-start | bytes 64
  473.1 24.2 %copy-start.2 = (bf16[1,5,256,256]{3,2,1,0:T(8,128)(2,1)S(1)}, bf16[1,5,256,256]{3,2,1,0:T(8,128)(2,1)}, u32[]{:S(2)}) copy-start(bf16[1,5,256,256]{3,2,1,0:T(8,128)(2,1)} %param.10) | copy-start | bytes 1966084
Sparse Core Ops, SparseCore 0:
  9.9 38.6 all-gather.1
  514.1 269.0 reduce-scatter.1
where the time goes:
time: 793 us; the launch traced here: 792 us
  waiting for transfers between devices  705 us (89%)
  matrix products  40.8 us (5%)
  starting transfers between devices  18.3 us (2%)
  between operations  15 us (2%)
  local copies, waits for them, and re-layouts  8.71 us (1%)
    ppermute x4, waiting for transfers between devices, shifted(): return lax.ppermute(array, axis, pairs)  397 us
    reduce_scatter x1, waiting for transfers between devices, per_device(): lax.psum_scatter(term_total, 'mpo', scatter_dimension=2, tiled=True)  269 us
    all_gather x1, waiting for transfers between devices, per_device(): full_block = lax.all_gather(live_block, 'mpo', axis=2, tiled=True)  38.7 us
    dot_general x1, matrix products, per_device(): jnp.einsum('tc,cvpq->tvpq', selector, stacked, preferred_element_type=jnp...  24.2 us
    ppermute x4, starting transfers between devices, shifted(): return lax.ppermute(array, axis, pairs)  18.3 us
    dot_general x1, matrix products, per_device(): jnp.einsum('tvpk,tqk->vpq', applied, right_terms, preferred_element_type=...  16.6 us
  transfers between devices with their start and end apart: 6, of which 5 were waited for; matrix products, arithmetic and copies ran while one was open for 1% of the time, Pallas kernels for 0%

commit v1 on v0

v1 whole, which is shorter than its diff:
```python
import functools

import jax
import jax.numpy as jnp
from jax import lax
from jax.experimental import pallas as pl
from jax.experimental.pallas import tpu as pltpu
from jax.sharding import PartitionSpec as P

SPINS = 8
MESH = pl.DeviceIdType.MESH
CHUNKS = 4
OWN, LOW, HIGH, FAR_LOW, FAR_HIGH, NOTHING = range(6)


def kernel(
    shift_ref, left_dim, right_dim, shift_any, wave, left, right, out,
    src0, src1, src2, src3, lbuf, rbuf, acc, rs_out, rs_in, shift2, slots,
    local_sem, pair_send, pair_recv, env_local, env_send, env_recv,
    z_send, z_recv, y_send, y_recv, x_send, xl, xr, rl, rr, rs_send, rs_recv,
):
    sources = (src0, src1, src2, src3)
    share, columns = wave.shape[1], wave.shape[2]
    terms = left.shape[0]
    m = lax.axis_index("mpo")
    s = lax.axis_index("sec")
    x, core = lax.div(m, 2), lax.rem(m, 2)
    y, z = lax.div(s, 16), lax.rem(s, 16)
    half, place = lax.div(z, 8), lax.rem(z, 8)
    other = 1 - core
    partner = 2 * x + other
    to_right, to_left = lax.rem(m + 2, 8), lax.rem(m + 6, 8)
    x_low, x_high = lax.rem(x + 3, 4), lax.rem(x + 1, 4)
    z_up = y * 16 + lax.rem(z + 7, 16)
    z_down = y * 16 + lax.rem(z + 9, 16)
    y_plus = lax.rem(y + 1, 4) * 16 + z
    y_minus = lax.rem(y + 3, 4) * 16 + z
    y_next = lax.rem(y + 1 + 2 * half, 4) * 16 + z

    def rows(start, count):
        return pl.ds(pl.multiple_of(start, share), count)

    mine = rows(m * share, share)
    block = rows(x * 2 * share, 2 * share)

    def send(src, dst, ssem, rsem, sec, mpo):
        pltpu.make_async_remote_copy(
            src_ref=src, dst_ref=dst, send_sem=ssem, recv_sem=rsem,
            device_id={"sec": sec, "mpo": mpo}, device_id_type=MESH,
        ).start()

    def await_bytes(ref, sem):
        pltpu.make_async_copy(ref, ref, sem).wait()

    own_vectors = pl.multiple_of(core * CHUNKS, CHUNKS)
    local = []
    for i in range(CHUNKS):
        local.append(
            pltpu.make_async_copy(
                wave.at[core * CHUNKS + i], sources[i].at[OWN, mine], local_sem.at[i]
            )
        )
    local.append(pltpu.make_async_copy(left, lbuf.at[pl.ds(0, terms)], env_local.at[0]))
    local.append(pltpu.make_async_copy(right, rbuf.at[pl.ds(0, terms)], env_local.at[1]))

    barrier = pltpu.get_barrier_semaphore()
    for core_id in range(2):
        for sec in (z_up, z_down):
            pl.semaphore_signal(
                barrier, inc=1, device_id={"sec": sec, "mpo": 2 * x + core_id},
                device_id_type=MESH,
            )
    for sec in (y_plus, y_minus):
        pl.semaphore_signal(
            barrier, inc=1, device_id={"sec": sec, "mpo": m}, device_id_type=MESH
        )
    for k in range(1, 8):
        pl.semaphore_signal(
            barrier, inc=1, device_id={"sec": s, "mpo": lax.rem(m + k, 8)},
            device_id_type=MESH,
        )
    for copy in local:
        copy.start()
    for i in range(CHUNKS):
        sources[i][NOTHING] = jnp.zeros(sources[i].shape[1:], sources[i].dtype)
    pl.semaphore_wait(barrier, 13)

    for i in range(CHUNKS):
        send(
            wave.at[other * CHUNKS + i], sources[i].at[OWN, mine],
            pair_send.at[i], pair_recv.at[i], s, partner,
        )
    for i in range(CHUNKS):
        for core_id in range(2):
            for slot, sec in ((LOW, z_up), (HIGH, z_down)):
                send(
                    wave.at[core_id * CHUNKS + i], sources[i].at[slot, mine],
                    z_send.at[i], z_recv.at[slot - LOW, i], sec, 2 * x + core_id,
                )
    send(shift_any, shift2, env_send.at[2], env_recv.at[2], s, partner)
    send(left, lbuf.at[pl.ds(terms, terms)], env_send.at[0], env_recv.at[0], s, partner)
    send(right, rbuf.at[pl.ds(terms, terms)], env_send.at[1], env_recv.at[1], s, partner)

    def x_start(slot, i):
        part = sources[i].at[slot, block]
        send(part, part, x_send.at[slot, i], xl.at[slot, i], s, to_right)
        send(part, part, x_send.at[slot, i], xr.at[slot, i], s, to_left)

    def x_relay(slot, i):
        low = rows(x_low * 2 * share, 2 * share)
        low_first = rows(x_low * 2 * share, share)
        await_bytes(sources[i].at[slot, low], xl.at[slot, i])
        part = sources[i].at[slot, low_first]
        send(part, part, x_send.at[slot, i], rl.at[slot, i], s, to_right)
        high = rows(x_high * 2 * share, 2 * share)
        high_last = rows(x_high * 2 * share + share, share)
        await_bytes(sources[i].at[slot, high], xr.at[slot, i])
        part = sources[i].at[slot, high_last]
        send(part, part, x_send.at[slot, i], rr.at[slot, i], s, to_left)

    def x_finish(slot, i):
        await_bytes(sources[i].at[slot, pl.ds(0, share)], rl.at[slot, i])
        await_bytes(sources[i].at[slot, pl.ds(0, share)], rr.at[slot, i])

    def product(i, first, last):
        @pl.loop(first, last)
        def _(t):
            applied = jnp.dot(
                lbuf[t], sources[i][slots[t]], preferred_element_type=jnp.float32
            ).astype(jnp.bfloat16)
            part = lax.dot_general(
                applied, rbuf[t], (((1,), (1,)), ((), ())),
                preferred_element_type=jnp.float32,
            )
            acc[...] += part

    def sums_start(i):
        for k in range(8):
            rs_out[i, k] = acc[pl.ds(k * share, share), :].astype(jnp.bfloat16)
        rs_in[x, core * CHUNKS + i] = acc[mine, :].astype(jnp.bfloat16)
        for k in range(1, 8):
            target = lax.rem(m + k, 8)
            send(
                rs_out.at[i, target], rs_in.at[x, core * CHUNKS + i],
                rs_send.at[i], rs_recv.at[i], s, target,
            )
        acc[...] = jnp.zeros_like(acc)

    row_ids = m * share + lax.broadcasted_iota(jnp.int32, (share, columns), 0)
    column_ids = lax.broadcasted_iota(jnp.int32, (share, columns), 1)
    keep = (row_ids < left_dim[0]) & (column_ids < right_dim[0])

    def sums_finish(i):
        await_bytes(rs_out.at[i, pl.ds(0, 7)], rs_recv.at[i])
        for v in (i, CHUNKS + i):
            total = rs_in[0, v].astype(jnp.float32)
            for k in range(1, 4):
                total = total + rs_in[k, v].astype(jnp.float32)
            out[v] = jnp.where(keep, total, jnp.zeros_like(total)).astype(out.dtype)

    for i in range(CHUNKS):
        local[i].wait()
        await_bytes(sources[i].at[OWN, mine], pair_recv.at[i])
        x_start(OWN, i)
    for i in range(CHUNKS):
        x_relay(OWN, i)
    acc[...] = jnp.zeros_like(acc)

    low_ok = place <= 6
    high_ok = place >= 1
    far_ok = jnp.where(half == 1, y <= 2, y >= 1)
    low_slot = jnp.where(low_ok, LOW, NOTHING)
    high_slot = jnp.where(high_ok, HIGH, NOTHING)
    far_low_slot = jnp.where(low_ok & far_ok, FAR_LOW, NOTHING)
    far_high_slot = jnp.where(high_ok & far_ok, FAR_HIGH, NOTHING)
    class_slots = (
        OWN,
        jnp.where(half == 1, high_slot, far_high_slot),
        jnp.where(half == 1, far_low_slot, low_slot),
        jnp.where(half == 1, low_slot, far_low_slot),
        jnp.where(half == 1, far_high_slot, high_slot),
    )

    def slot_of(shift):
        found = jnp.int32(OWN)
        for c in range(1, 5):
            found = jnp.where(shift == c, class_slots[c], found)
        return found

    await_bytes(shift2, env_recv.at[2])
    for t in range(terms):
        slots[t] = slot_of(shift_ref[t])
        slots[terms + t] = slot_of(shift2[t])

    for i in range(CHUNKS):
        for slot in (LOW, HIGH):
            await_bytes(sources[i].at[slot, block], z_recv.at[slot - LOW, i])
            part = sources[i].at[slot, block]
            send(
                part, sources[i].at[slot + 2, block],
                y_send.at[i], y_recv.at[slot - LOW, i], y_next, m,
            )
            x_start(slot, i)
        if i == 1:
            local[CHUNKS].wait()
            local[CHUNKS + 1].wait()
            await_bytes(lbuf.at[pl.ds(terms, terms)], env_recv.at[0])
            await_bytes(rbuf.at[pl.ds(terms, terms)], env_recv.at[1])
        if i > 0:
            product(i - 1, 0, terms)
        for slot in (LOW, HIGH):
            x_relay(slot, i)
        for slot in (FAR_LOW, FAR_HIGH):
            await_bytes(sources[i].at[slot, block], y_recv.at[slot - FAR_LOW, i])
            x_start(slot, i)
        if i > 0:
            product(i - 1, terms, 2 * terms)
            sums_start(i - 1)
        for slot in (FAR_LOW, FAR_HIGH):
            x_relay(slot, i)
        for slot in range(5):
            x_finish(slot, i)
        if i > 1:
            sums_finish(i - 2)
    product(CHUNKS - 1, 0, 2 * terms)
    sums_start(CHUNKS - 1)
    sums_finish(CHUNKS - 2)
    sums_finish(CHUNKS - 1)

    for i in range(CHUNKS):
        await_bytes(sources[i].at[OWN, pl.ds(0, share)], pair_send.at[i])
        await_bytes(sources[i].at[OWN, pl.ds(0, 4 * share)], z_send.at[i])
        await_bytes(sources[i].at[OWN, pl.ds(0, 4 * share)], y_send.at[i])
        await_bytes(rs_out.at[i, pl.ds(0, 7)], rs_send.at[i])
        for slot in range(5):
            await_bytes(sources[i].at[slot, pl.ds(0, 6 * share)], x_send.at[slot, i])
    await_bytes(lbuf.at[pl.ds(0, terms)], env_send.at[0])
    await_bytes(rbuf.at[pl.ds(0, terms)], env_send.at[1])
    await_bytes(shift2, env_send.at[2])


def per_device(wavefunction, left_env, right_env, left_dims, right_dims, term_shift):
    _, vectors, share, columns = wavefunction.shape
    full = left_env.shape[2]
    terms = left_env.shape[1]
    rows_here = lax.axis_index("mpo") * share + jnp.arange(share, dtype=jnp.int32)
    column_ids = jnp.arange(columns, dtype=jnp.int32)
    keep = (rows_here[:, None] < left_dims[0]) & (column_ids[None, :] < right_dims[0])
    live = jnp.where(keep[None], wavefunction[0], jnp.zeros_like(wavefunction[0]))
    smem = pl.BlockSpec(memory_space=pltpu.SMEM)
    anywhere = pl.BlockSpec(memory_space=pl.ANY)
    bf16 = jnp.bfloat16
    dma = pltpu.SemaphoreType.DMA
    out = pl.pallas_call(
        kernel,
        out_shape=jax.ShapeDtypeStruct((vectors, share, columns), bf16),
        in_specs=[smem, smem, smem, anywhere, anywhere, anywhere, anywhere],
        out_specs=pl.BlockSpec(memory_space=pltpu.VMEM),
        scratch_shapes=[pltpu.VMEM((6, full, columns), bf16) for _ in range(CHUNKS)]
        + [
            pltpu.VMEM((2 * terms, full, full), bf16),
            pltpu.VMEM((2 * terms, columns, columns), bf16),
            pltpu.VMEM((full, columns), jnp.float32),
            pltpu.VMEM((CHUNKS, 8, share, columns), bf16),
            pltpu.VMEM((4, vectors, share, columns), bf16),
            pltpu.SMEM((terms,), jnp.int32),
            pltpu.SMEM((2 * terms,), jnp.int32),
            dma((CHUNKS,)), dma((CHUNKS,)), dma((CHUNKS,)),
            dma((2,)), dma((3,)), dma((3,)),
            dma((CHUNKS,)), dma((2, CHUNKS)), dma((CHUNKS,)), dma((2, CHUNKS)),
            dma((5, CHUNKS)), dma((5, CHUNKS)), dma((5, CHUNKS)),
            dma((5, CHUNKS)), dma((5, CHUNKS)),
            dma((CHUNKS,)), dma((CHUNKS,)),
        ],
        compiler_params=pltpu.CompilerParams(
            collective_id=0, has_side_effects=True, vmem_limit_bytes=60 * 1024 * 1024
        ),
    )(term_shift, left_dims, right_dims, term_shift, live, left_env[0], right_env[0])
    return out[None]


def solution(mesh):
    in_specs = (
        P("sec", None, "mpo", None),
        P("sec", "mpo", None, None),
        P("sec", "mpo", None, None),
        P("sec"),
        P("sec"),
        P("mpo"),
    )
    out_specs = P("sec", None, "mpo", None)
    return jax.shard_map(
        per_device, mesh=mesh, in_specs=in_specs, out_specs=out_specs, check_vma=False
    )
```

time: 793 us -> 112 us (0.14)
  the two profiles are of different devices: /device:TPU:1 before, /device:TPU:97 now
where the time goes in v1:
time: 112 us
  Pallas kernels  107 us (96%)
  other arithmetic  1.76 us (2%)
  local copies, waits for them, and re-layouts  1.67 us (1%)
  between operations  1.33 us (1%)
    pallas_call x1, Pallas kernels, per_device(): pl.pallas_call(kernel, out_shape=jax.ShapeDtypeStruct((vectors, share, co...  107 us

profile of v1, /device:TPU:97, one launch (start us, length us, event | category | flops | bytes accessed | tf_op | source)
XLA Modules:
  0.0 111.8 jit_solution(15006501333215159310)
XLA Ops:
  1.3 0.1 broadcast_and_fusion
  1.4 1.7 %bitcast_select_fusion.wave = bf16[8,64,256]{2,1,0:T(8,128)(2,1)} fusion(bf16[1,8,64,256]{3,2,1,0:T(8,128)(2,1)} %param.6, pred[64,256]{1,0:T(8,128)(4,1)S(1)} %broadcast_and_fusion), kind=kLoop, calls=%fused_computation | loop fusion | flops 131072 | bytes 540672 | tf_op jit(solution)/shard_map/jit(_where)/select_n | solution.py:249
  3.1 107.0 %shard_map.64 = bf16[8,64,256]{2,1,0:T(8,128)(2,1)} custom-call(s32[5]{0:T(128)} %shift_any.1, s32[1]{0:T(128)} %copy.8.left_dim, s32[1]{0:T(128)} %copy.9.right_dim, s32[5]{0:T(128)} %shift_any.1, bf16[8,64,256]{2,1,0:T(8,128)(2,1)} %bitcast_select_fusion.wave, bf16[5,512,512]{2,1,0:T(8,128)(2,1)} %bitcast.9, bf16[5,256,256]{2,1,0:T(8,128)(2,1)} %bitcast.11), custom_call_target="tpu_custom_call" | custom-call | tf_op jit(solution)/shard_map/pallas_call | solution.py:254
  110.1 1.7 %copy.10 = bf16[1,8,64,256]{3,2,1,0:T(8,128)(2,1)} copy(bf16[1,8,64,256]{3,2,1,0:T(8,128)(2,1)} %bitcast.10) | data formatting | bytes 524288
  (2 shorter events, 0.0 us)

commit v2 on v1

v2 whole, which is shorter than its diff:
```python
import jax
import jax.numpy as jnp
from jax import lax
from jax.experimental import pallas as pl
from jax.experimental.pallas import tpu as pltpu
from jax.sharding import PartitionSpec as P

SPINS = 8
MESH = pl.DeviceIdType.MESH
CHUNKS = 4
OWN, LOW, HIGH, FAR_LOW, FAR_HIGH, NOTHING = range(6)
FROM_LOW, FROM_HIGH, REST = range(3)
GATHER_FIRST = frozenset((LOW, i) for i in range(CHUNKS))
PACE = 2
FIRST_NEAR = 9.5
CHUNK_TIME = 6.5
RELAYED = 4.0
ACROSS = 3.0
FIRST_OWN = 3.0
PIECES = 5


def kernel(
    shift_ref, left_dim, right_dim, shift_any, wave, left, right, out,
    src0, src1, src2, src3, lbuf, rbuf, acc, rs_out, rs_in, shift2, slots,
    local_sem, pair_send, pair_recv, env_local, env_send, env_recv,
    z_send, z_recv, y_send, y_recv, x_send, x_recv, rs_send, rs_recv,
):
    sources = (src0, src1, src2, src3)
    share, columns = wave.shape[1], wave.shape[2]
    terms = left.shape[0]
    m = lax.axis_index("mpo")
    s = lax.axis_index("sec")
    x, core = lax.div(m, 2), lax.rem(m, 2)
    y, z = lax.div(s, 16), lax.rem(s, 16)
    half, place = lax.div(z, 8), lax.rem(z, 8)
    other = 1 - core
    partner = 2 * x + other
    to_right, to_left = lax.rem(m + 2, 8), lax.rem(m + 6, 8)
    x_low, x_high, x_far = lax.rem(x + 3, 4), lax.rem(x + 1, 4), lax.rem(x + 2, 4)

    def along_z(step):
        return y * 16 + lax.rem(z + step + 16, 16)

    z_first = along_z(7 - 14 * core)
    y_plus = lax.rem(y + 1, 4) * 16 + z
    y_minus = lax.rem(y + 3, 4) * 16 + z
    y_next = lax.rem(y + 1 + 2 * half, 4) * 16 + z

    def rows(start, count):
        return pl.ds(pl.multiple_of(start, share), count)

    def piece(chip, side):
        return rows((2 * chip + side) * share, share)

    mine = rows(m * share, share)

    def send(src, dst, ssem, rsem, sec, mpo):
        pltpu.make_async_remote_copy(
            src_ref=src, dst_ref=dst, send_sem=ssem, recv_sem=rsem,
            device_id={"sec": sec, "mpo": mpo}, device_id_type=MESH,
        ).start()

    def await_bytes(ref, sem):
        pltpu.make_async_copy(ref, ref, sem).wait()

    local = []
    for i in range(CHUNKS):
        local.append(
            pltpu.make_async_copy(
                wave.at[core * CHUNKS + i], sources[i].at[OWN, mine], local_sem.at[i]
            )
        )
    local.append(pltpu.make_async_copy(left, lbuf.at[pl.ds(0, terms)], env_local.at[0]))
    local.append(pltpu.make_async_copy(right, rbuf.at[pl.ds(0, terms)], env_local.at[1]))

    barrier = pltpu.get_barrier_semaphore()

    def greet(sec, mpo):
        pl.semaphore_signal(
            barrier, inc=1, device_id={"sec": sec, "mpo": mpo}, device_id_type=MESH
        )

    for step in (7, -7):
        for core_id in range(2):
            greet(along_z(step), 2 * x + core_id)
    for sec in (along_z(2), along_z(-2), y_plus, y_minus):
        greet(sec, m)
    for k in range(1, 8):
        greet(s, lax.rem(m + k, 8))
    for copy in local:
        copy.start()
    for i in range(CHUNKS):
        sources[i][NOTHING] = jnp.zeros(sources[i].shape[1:], sources[i].dtype)
    acc[...] = jnp.zeros_like(acc)

    low_ok = place <= 6
    high_ok = place >= 1
    far_ok = jnp.where(half == 1, y <= 2, y >= 1)
    low_slot = jnp.where(low_ok, LOW, NOTHING)
    high_slot = jnp.where(high_ok, HIGH, NOTHING)
    far_low_slot = jnp.where(low_ok & far_ok, FAR_LOW, NOTHING)
    far_high_slot = jnp.where(high_ok & far_ok, FAR_HIGH, NOTHING)
    class_slots = (
        OWN,
        jnp.where(half == 1, high_slot, far_high_slot),
        jnp.where(half == 1, far_low_slot, low_slot),
        jnp.where(half == 1, low_slot, far_low_slot),
        jnp.where(half == 1, far_high_slot, high_slot),
    )

    def slot_of(shift):
        found = jnp.int32(OWN)
        for c in range(1, 5):
            found = jnp.where(shift == c, class_slots[c], found)
        return found

    row_ids = m * share + lax.broadcasted_iota(jnp.int32, (share, columns), 0)
    column_ids = lax.broadcasted_iota(jnp.int32, (share, columns), 1)
    keep = (row_ids < left_dim[0]) & (column_ids < right_dim[0])
    pl.semaphore_wait(barrier, 15)

    def z_start(i):
        @pl.when(core == 0)
        def _():
            for core_id in range(2):
                send(
                    wave.at[core_id * CHUNKS + i], sources[i].at[LOW, mine],
                    z_send.at[i], z_recv.at[0, 0, i], along_z(7), 2 * x + core_id,
                )

        @pl.when(core == 1)
        def _():
            for core_id in range(2):
                send(
                    wave.at[core_id * CHUNKS + i], sources[i].at[HIGH, mine],
                    z_send.at[i], z_recv.at[1, 1, i], along_z(-7), 2 * x + core_id,
                )

    for i in range(PACE):
        z_start(i)
    for i in range(CHUNKS):
        send(
            wave.at[other * CHUNKS + i], sources[i].at[OWN, mine],
            pair_send.at[i], pair_recv.at[i], s, partner,
        )
    send(shift_any, shift2, env_send.at[2], env_recv.at[2], s, partner)
    send(left, lbuf.at[pl.ds(terms, terms)], env_send.at[0], env_recv.at[0], s, partner)
    send(right, rbuf.at[pl.ds(terms, terms)], env_send.at[1], env_recv.at[1], s, partner)

    def x_part(slot, i, part, to, role):
        send(part, part, x_send.at[slot, i], x_recv.at[role, slot, i], s, to)

    def y_part(slot, i, which):
        send(
            sources[i].at[slot, which], sources[i].at[slot + 2, which],
            y_send.at[slot - LOW, i], y_recv.at[slot - LOW, 0, i], y_next, m,
        )

    def x_start(slot, i, side):
        part = sources[i].at[slot, piece(x, side)]
        x_part(slot, i, part, to_right, FROM_LOW if side == 0 else REST)
        x_part(slot, i, part, to_left, FROM_HIGH if side == 1 else REST)

    def x_relay(slot, i):
        for side, chip, to in ((0, x_low, to_right), (1, x_high, to_left)):
            part = sources[i].at[slot, piece(chip, side)]
            await_bytes(part, x_recv.at[side, slot, i])
            x_part(slot, i, part, to, REST)
            if (slot, i) in GATHER_FIRST:
                y_part(slot, i, piece(chip, side))

    def x_finish(slot, i):
        await_bytes(sources[i].at[slot, pl.ds(0, 4 * share)], x_recv.at[REST, slot, i])
        if (slot, i) in GATHER_FIRST:
            y_part(slot, i, piece(x_low, 1))
            y_part(slot, i, piece(x_high, 0))
            y_part(slot, i, rows(2 * x_far * share, 2 * share))

    def own_start(i):
        local[i].wait()
        await_bytes(sources[i].at[OWN, mine], pair_recv.at[i])
        x_start(OWN, i, 0)
        x_start(OWN, i, 1)

    def near_start(slot, side, i):
        await_bytes(sources[i].at[slot, piece(x, side)], z_recv.at[slot - LOW, side, i])
        which = piece(x, side)
        if slot - LOW == side:
            send(
                sources[i].at[slot, which], sources[i].at[LOW + HIGH - slot, which],
                z_send.at[i], z_recv.at[1 - side, side, i],
                along_z(2 - 4 * side), m,
            )
        if (slot, i) in GATHER_FIRST:
            y_part(slot, i, which)
        else:
            send(
                sources[i].at[slot, which], sources[i].at[slot + 2, which],
                y_send.at[slot - LOW, i], y_recv.at[slot - LOW, side, i], y_next, m,
            )
        x_start(slot, i, side)

    def far_start(slot, side, i):
        await_bytes(
            sources[i].at[slot + 2, piece(x, side)], y_recv.at[slot - LOW, side, i]
        )
        x_start(slot + 2, i, side)

    def far_finish(slot, i):
        await_bytes(sources[i].at[slot + 2], y_recv.at[slot - LOW, 0, i])

    def env_ready():
        await_bytes(shift2, env_recv.at[2])
        for t in range(terms):
            slots[t] = slot_of(shift_ref[t])
            slots[terms + t] = slot_of(shift2[t])
        local[CHUNKS].wait()
        local[CHUNKS + 1].wait()
        await_bytes(lbuf.at[pl.ds(terms, terms)], env_recv.at[0])
        await_bytes(rbuf.at[pl.ds(terms, terms)], env_recv.at[1])

    def product(i, first, last):
        for t in range(first, last):
            applied = jnp.dot(
                lbuf[t], sources[i][slots[t]], preferred_element_type=jnp.float32
            ).astype(jnp.bfloat16)
            acc[...] += lax.dot_general(
                applied, rbuf[t], (((1,), (1,)), ((), ())),
                preferred_element_type=jnp.float32,
            )

    def sums_start(i):
        for k in range(8):
            rs_out[i, k] = acc[pl.ds(k * share, share), :].astype(jnp.bfloat16)
        rs_in[x, core * CHUNKS + i] = acc[mine, :].astype(jnp.bfloat16)
        for k in range(1, 8):
            target = lax.rem(m + k, 8)
            send(
                rs_out.at[i, target], rs_in.at[x, core * CHUNKS + i],
                rs_send.at[i], rs_recv.at[i], s, target,
            )
        acc[...] = jnp.zeros_like(acc)

    def sums_finish(i):
        await_bytes(rs_out.at[i, pl.ds(0, 7)], rs_recv.at[i])
        for v in (i, CHUNKS + i):
            total = rs_in[0, v].astype(jnp.float32)
            for k in range(1, 4):
                total = total + rs_in[k, v].astype(jnp.float32)
            out[v] = jnp.where(keep, total, jnp.zeros_like(total)).astype(out.dtype)

    plan = []

    def at(when, function, *operands):
        plan.append((when, len(plan), function, operands))

    done = 0.0
    for i in range(CHUNKS):
        at(0.1 * i, own_start, i)
        at(FIRST_OWN + 2.1 * i, x_relay, OWN, i)
        base = FIRST_NEAR + CHUNK_TIME * i
        rel = base + RELAYED
        at(base, near_start, LOW, 0, i)
        at(base, near_start, HIGH, 1, i)
        if i + PACE < CHUNKS:
            at(base, z_start, i + PACE)
        at(rel, near_start, LOW, 1, i)
        at(rel, near_start, HIGH, 0, i)
        ready = rel + 8
        for slot in (LOW, HIGH):
            at(rel + 3, x_relay, slot, i)
            if (slot, i) in GATHER_FIRST:
                at(rel + 6, x_finish, slot, i)
                ready = max(ready, rel + 14)
            else:
                first = 0 if slot == LOW else 1
                at(base + ACROSS, far_start, slot, first, i)
                at(rel + ACROSS, far_start, slot, 1 - first, i)
                at(rel + ACROSS + 4, x_relay, slot + 2, i)
                ready = max(ready, rel + ACROSS + 8)
        done = max(done + 5.0, ready)
        at(done, x_finish, OWN, i)
        for slot in (LOW, HIGH):
            if (slot, i) in GATHER_FIRST:
                at(done, far_finish, slot, i)
            else:
                at(done, x_finish, slot, i)
                at(done, x_finish, slot + 2, i)
        if i == 0:
            at(done, env_ready)
        for k in range(PIECES):
            at(
                done + 5.0 * k / PIECES, product, i,
                2 * terms * k // PIECES, 2 * terms * (k + 1) // PIECES,
            )
        at(done + 4.9, sums_start, i)
        at(done + 100.0, sums_finish, i)
    for _, _, function, operands in sorted(plan, key=lambda entry: entry[:2]):
        function(*operands)

    for i in range(CHUNKS):
        await_bytes(sources[i].at[OWN, pl.ds(0, share)], pair_send.at[i])
        await_bytes(sources[i].at[OWN, pl.ds(0, 4 * share)], z_send.at[i])
        await_bytes(rs_out.at[i, pl.ds(0, 7)], rs_send.at[i])
        await_bytes(sources[i].at[OWN, pl.ds(0, 6 * share)], x_send.at[OWN, i])
        for slot in (LOW, HIGH):
            await_bytes(sources[i].at[slot, pl.ds(0, 6 * share)], x_send.at[slot, i])
            if (slot, i) in GATHER_FIRST:
                await_bytes(sources[i].at[slot], y_send.at[slot - LOW, i])
            else:
                await_bytes(
                    sources[i].at[slot, pl.ds(0, 2 * share)], y_send.at[slot - LOW, i]
                )
                await_bytes(
                    sources[i].at[slot, pl.ds(0, 6 * share)], x_send.at[slot + 2, i]
                )
    await_bytes(lbuf.at[pl.ds(0, terms)], env_send.at[0])
    await_bytes(rbuf.at[pl.ds(0, terms)], env_send.at[1])
    await_bytes(shift2, env_send.at[2])


def per_device(wavefunction, left_env, right_env, left_dims, right_dims, term_shift):
    _, vectors, share, columns = wavefunction.shape
    full = left_env.shape[2]
    terms = left_env.shape[1]
    rows_here = lax.axis_index("mpo") * share + jnp.arange(share, dtype=jnp.int32)
    column_ids = jnp.arange(columns, dtype=jnp.int32)
    keep = (rows_here[:, None] < left_dims[0]) & (column_ids[None, :] < right_dims[0])
    live = jnp.where(keep[None], wavefunction[0], jnp.zeros_like(wavefunction[0]))
    smem = pl.BlockSpec(memory_space=pltpu.SMEM)
    anywhere = pl.BlockSpec(memory_space=pl.ANY)
    bf16 = jnp.bfloat16
    dma = pltpu.SemaphoreType.DMA
    out = pl.pallas_call(
        kernel,
        out_shape=jax.ShapeDtypeStruct((vectors, share, columns), bf16),
        in_specs=[smem, smem, smem, anywhere, anywhere, anywhere, anywhere],
        out_specs=pl.BlockSpec(memory_space=pltpu.VMEM),
        scratch_shapes=[pltpu.VMEM((6, full, columns), bf16) for _ in range(CHUNKS)]
        + [
            pltpu.VMEM((2 * terms, full, full), bf16),
            pltpu.VMEM((2 * terms, columns, columns), bf16),
            pltpu.VMEM((full, columns), jnp.float32),
            pltpu.VMEM((CHUNKS, 8, share, columns), bf16),
            pltpu.VMEM((4, vectors, share, columns), bf16),
            pltpu.SMEM((terms,), jnp.int32),
            pltpu.SMEM((2 * terms,), jnp.int32),
            dma((CHUNKS,)), dma((CHUNKS,)), dma((CHUNKS,)),
            dma((2,)), dma((3,)), dma((3,)),
            dma((CHUNKS,)), dma((2, 2, CHUNKS)), dma((2, CHUNKS)), dma((2, 2, CHUNKS)),
            dma((5, CHUNKS)), dma((3, 5, CHUNKS)),
            dma((CHUNKS,)), dma((CHUNKS,)),
        ],
        compiler_params=pltpu.CompilerParams(
            collective_id=0, has_side_effects=True, vmem_limit_bytes=60 * 1024 * 1024
        ),
    )(term_shift, left_dims, right_dims, term_shift, live, left_env[0], right_env[0])
    return out[None]


def solution(mesh):
    in_specs = (
        P("sec", None, "mpo", None),
        P("sec", "mpo", None, None),
        P("sec", "mpo", None, None),
        P("sec"),
        P("sec"),
        P("mpo"),
    )
    out_specs = P("sec", None, "mpo", None)
    return jax.shard_map(
        per_device, mesh=mesh, in_specs=in_specs, out_specs=out_specs, check_vma=False
    )
```

time: 112 us -> 84.9 us (0.76)
  the two profiles are of different devices: /device:TPU:97 before, /device:TPU:1 now
where the time goes in v2:
time: 84.9 us; the launch traced here: 84.7 us
  Pallas kernels  79.9 us (94%)
  other arithmetic  1.76 us (2%)
  local copies, waits for them, and re-layouts  1.67 us (2%)
  between operations  1.33 us (2%)
    pallas_call x1, Pallas kernels, per_device(): pl.pallas_call(kernel, out_shape=jax.ShapeDtypeStruct((vectors, share, co...  79.9 us

profile of v2, /device:TPU:1, one launch (start us, length us, event | category | flops | bytes accessed | tf_op | source)
XLA Modules:
  0.0 84.7 jit_solution(13817581187295891808)
XLA Ops:
  1.3 0.1 broadcast_and_fusion
  1.4 1.7 %bitcast_select_fusion.wave = bf16[8,64,256]{2,1,0:T(8,128)(2,1)} fusion(bf16[1,8,64,256]{3,2,1,0:T(8,128)(2,1)} %param.6, pred[64,256]{1,0:T(8,128)(4,1)S(1)} %broadcast_and_fusion), kind=kLoop, calls=%fused_computation | loop fusion | flops 131072 | bytes 540672 | tf_op jit(solution)/shard_map/jit(_where)/select_n | solution.py:330
  3.1 79.9 %shard_map.64 = bf16[8,64,256]{2,1,0:T(8,128)(2,1)} custom-call(s32[5]{0:T(128)} %shift_any.1, s32[1]{0:T(128)} %copy.8.left_dim, s32[1]{0:T(128)} %copy.9.right_dim, s32[5]{0:T(128)} %shift_any.1, bf16[8,64,256]{2,1,0:T(8,128)(2,1)} %bitcast_select_fusion.wave, bf16[5,512,512]{2,1,0:T(8,128)(2,1)} %bitcast.9, bf16[5,256,256]{2,1,0:T(8,128)(2,1)} %bitcast.11), custom_call_target="tpu_custom_call" | custom-call | tf_op jit(solution)/shard_map/pallas_call | solution.py:335
  83.0 1.7 %copy.10 = bf16[1,8,64,256]{3,2,1,0:T(8,128)(2,1)} copy(bf16[1,8,64,256]{3,2,1,0:T(8,128)(2,1)} %bitcast.10) | data formatting | bytes 524288
  (2 shorter events, 0.0 us)

commit v3 on v2

--- a/solution.py
+++ b/solution.py
@@ -13,21 +13,24 @@
 GATHER_FIRST = frozenset((LOW, i) for i in range(CHUNKS))
 PACE = 2
 FIRST_NEAR = 9.5
-CHUNK_TIME = 6.5
+CHUNK_TIME = 4.5
 RELAYED = 4.0
 ACROSS = 3.0
 FIRST_OWN = 3.0
-PIECES = 5
+FAR_READY = 11.0
+PACE_DELAY = 0.0
+PRODUCT_TIME = 2.7
+PIECES = 2
 
 
 def kernel(
-    shift_ref, left_dim, right_dim, shift_any, wave, left, right, out,
-    src0, src1, src2, src3, lbuf, rbuf, acc, rs_out, rs_in, shift2, slots,
+    shift_ref, left_dim, right_dim, shift_any, raw_any, left, right, out,
+    wave, src0, src1, src2, src3, lbuf, rbuf, acc, rs_out, rs_in, shift2, slots,
     local_sem, pair_send, pair_recv, env_local, env_send, env_recv,
     z_send, z_recv, y_send, y_recv, x_send, x_recv, rs_send, rs_recv,
 ):
     sources = (src0, src1, src2, src3)
-    share, columns = wave.shape[1], wave.shape[2]
+    share, columns = raw_any.shape[1], raw_any.shape[2]
     terms = left.shape[0]
     m = lax.axis_index("mpo")
     s = lax.axis_index("sec")
@@ -64,13 +67,9 @@
     def await_bytes(ref, sem):
         pltpu.make_async_copy(ref, ref, sem).wait()
 
+    load = pltpu.make_async_copy(raw_any, wave, local_sem.at[0])
+    load.start()
     local = []
-    for i in range(CHUNKS):
-        local.append(
-            pltpu.make_async_copy(
-                wave.at[core * CHUNKS + i], sources[i].at[OWN, mine], local_sem.at[i]
-            )
-        )
     local.append(pltpu.make_async_copy(left, lbuf.at[pl.ds(0, terms)], env_local.at[0]))
     local.append(pltpu.make_async_copy(right, rbuf.at[pl.ds(0, terms)], env_local.at[1]))
 
@@ -118,6 +117,11 @@
     row_ids = m * share + lax.broadcasted_iota(jnp.int32, (share, columns), 0)
     column_ids = lax.broadcasted_iota(jnp.int32, (share, columns), 1)
     keep = (row_ids < left_dim[0]) & (column_ids < right_dim[0])
+    load.wait()
+    for v in range(2 * CHUNKS):
+        wave[v] = jnp.where(keep, wave[v], jnp.zeros_like(wave[v]))
+    for i in range(CHUNKS):
+        sources[i][OWN, mine] = wave[core * CHUNKS + i]
     pl.semaphore_wait(barrier, 15)
 
     def z_start(i):
@@ -178,7 +182,6 @@
             y_part(slot, i, rows(2 * x_far * share, 2 * share))
 
     def own_start(i):
-        local[i].wait()
         await_bytes(sources[i].at[OWN, mine], pair_recv.at[i])
         x_start(OWN, i, 0)
         x_start(OWN, i, 1)
@@ -215,8 +218,8 @@
         for t in range(terms):
             slots[t] = slot_of(shift_ref[t])
             slots[terms + t] = slot_of(shift2[t])
-        local[CHUNKS].wait()
-        local[CHUNKS + 1].wait()
+        local[0].wait()
+        local[1].wait()
         await_bytes(lbuf.at[pl.ds(terms, terms)], env_recv.at[0])
         await_bytes(rbuf.at[pl.ds(terms, terms)], env_recv.at[1])
 
@@ -234,7 +237,7 @@
         for k in range(8):
             rs_out[i, k] = acc[pl.ds(k * share, share), :].astype(jnp.bfloat16)
         rs_in[x, core * CHUNKS + i] = acc[mine, :].astype(jnp.bfloat16)
-        for k in range(1, 8):
+        for k in (4, 5, 3, 2, 6, 7, 1):
             target = lax.rem(m + k, 8)
             send(
                 rs_out.at[i, target], rs_in.at[x, core * CHUNKS + i],
@@ -264,7 +267,7 @@
         at(base, near_start, LOW, 0, i)
         at(base, near_start, HIGH, 1, i)
         if i + PACE < CHUNKS:
-            at(base, z_start, i + PACE)
+            at(base + PACE_DELAY, z_start, i + PACE)
         at(rel, near_start, LOW, 1, i)
         at(rel, near_start, HIGH, 0, i)
         ready = rel + 8
@@ -272,14 +275,14 @@
             at(rel + 3, x_relay, slot, i)
             if (slot, i) in GATHER_FIRST:
                 at(rel + 6, x_finish, slot, i)
-                ready = max(ready, rel + 14)
+                ready = max(ready, rel + FAR_READY)
             else:
                 first = 0 if slot == LOW else 1
                 at(base + ACROSS, far_start, slot, first, i)
                 at(rel + ACROSS, far_start, slot, 1 - first, i)
                 at(rel + ACROSS + 4, x_relay, slot + 2, i)
                 ready = max(ready, rel + ACROSS + 8)
-        done = max(done + 5.0, ready)
+        done = max(done + PRODUCT_TIME, ready)
         at(done, x_finish, OWN, i)
         for slot in (LOW, HIGH):
             if (slot, i) in GATHER_FIRST:
@@ -291,10 +294,10 @@
             at(done, env_ready)
         for k in range(PIECES):
             at(
-                done + 5.0 * k / PIECES, product, i,
+                done + PRODUCT_TIME * k / PIECES, product, i,
                 2 * terms * k // PIECES, 2 * terms * (k + 1) // PIECES,
             )
-        at(done + 4.9, sums_start, i)
+        at(done + PRODUCT_TIME - 0.1, sums_start, i)
         at(done + 100.0, sums_finish, i)
     for _, _, function, operands in sorted(plan, key=lambda entry: entry[:2]):
         function(*operands)
@@ -324,10 +327,6 @@
     _, vectors, share, columns = wavefunction.shape
     full = left_env.shape[2]
     terms = left_env.shape[1]
-    rows_here = lax.axis_index("mpo") * share + jnp.arange(share, dtype=jnp.int32)
-    column_ids = jnp.arange(columns, dtype=jnp.int32)
-    keep = (rows_here[:, None] < left_dims[0]) & (column_ids[None, :] < right_dims[0])
-    live = jnp.where(keep[None], wavefunction[0], jnp.zeros_like(wavefunction[0]))
     smem = pl.BlockSpec(memory_space=pltpu.SMEM)
     anywhere = pl.BlockSpec(memory_space=pl.ANY)
     bf16 = jnp.bfloat16
@@ -337,7 +336,8 @@
         out_shape=jax.ShapeDtypeStruct((vectors, share, columns), bf16),
         in_specs=[smem, smem, smem, anywhere, anywhere, anywhere, anywhere],
         out_specs=pl.BlockSpec(memory_space=pltpu.VMEM),
-        scratch_shapes=[pltpu.VMEM((6, full, columns), bf16) for _ in range(CHUNKS)]
+        scratch_shapes=[pltpu.VMEM((vectors, share, columns), bf16)]
+        + [pltpu.VMEM((6, full, columns), bf16) for _ in range(CHUNKS)]
         + [
             pltpu.VMEM((2 * terms, full, full), bf16),
             pltpu.VMEM((2 * terms, columns, columns), bf16),
@@ -346,7 +346,7 @@
             pltpu.VMEM((4, vectors, share, columns), bf16),
             pltpu.SMEM((terms,), jnp.int32),
             pltpu.SMEM((2 * terms,), jnp.int32),
-            dma((CHUNKS,)), dma((CHUNKS,)), dma((CHUNKS,)),
+            dma((1,)), dma((CHUNKS,)), dma((CHUNKS,)),
             dma((2,)), dma((3,)), dma((3,)),
             dma((CHUNKS,)), dma((2, 2, CHUNKS)), dma((2, CHUNKS)), dma((2, 2, CHUNKS)),
             dma((5, CHUNKS)), dma((3, 5, CHUNKS)),
@@ -355,7 +355,7 @@
         compiler_params=pltpu.CompilerParams(
             collective_id=0, has_side_effects=True, vmem_limit_bytes=60 * 1024 * 1024
         ),
-    )(term_shift, left_dims, right_dims, term_shift, live, left_env[0], right_env[0])
+    )(term_shift, left_dims, right_dims, term_shift, wavefunction[0], left_env[0], right_env[0])
     return out[None]
 
 

time: 84.9 us -> 78.8 us (0.928)
  Pallas kernels: 79.9 us -> 74.8 us
  other arithmetic: 1.76 us -> 0 us
    pallas_call x1, Pallas kernels: 79.9 us -> 74.8 us  [per_device(): pl.pallas_call(kernel, out_shape=jax.ShapeDtypeStruct((vectors, share, co...]
    select_n x1 -> x0, other arithmetic: 1.67 us -> none  [per_device(): jnp.where(keep[None], wavefunction[0], jnp.zeros_like(wavefunction[0]))]
where the time goes in v3:
time: 78.8 us; the launch traced here: 77.8 us
  Pallas kernels  74.8 us (95%)
  local copies, waits for them, and re-layouts  1.67 us (2%)
  between operations  1.3 us (2%)
    pallas_call x1, Pallas kernels, per_device(): pl.pallas_call(kernel, out_shape=jax.ShapeDtypeStruct((vectors, share, co...  74.8 us
    unnamed x1, local copies, waits for them, and re-layouts  1.67 us

profile of v3, /device:TPU:1, one launch (start us, length us, event | category | flops | bytes accessed | tf_op | source)
XLA Modules:
  0.0 77.8 jit_solution(13438800972409172813)
XLA Ops:
  1.3 74.8 %shard_map.64 = bf16[8,64,256]{2,1,0:T(8,128)(2,1)} custom-call(s32[5]{0:T(128)} %shift_any.1, s32[1]{0:T(128)S(6)} %copy.8.left_dim, s32[1]{0:T(128)S(6)} %copy.9.right_dim, s32[5]{0:T(128)} %shift_any.1, bf16[8,64,256]{2,1,0:T(8,128)(2,1)} %bitcast.7, bf16[5,512,512]{2,1,0:T(8,128)(2,1)} %bitcast.4, bf16[5,256,256]{2,1,0:T(8,128)(2,1)} %bitcast.6), custom_call_target="tpu_custom_call" | custom-call | tf_op jit(solution)/shard_map/pallas_call | solution.py:334
  76.1 1.7 %copy.10 = bf16[1,8,64,256]{3,2,1,0:T(8,128)(2,1)} copy(bf16[1,8,64,256]{3,2,1,0:T(8,128)(2,1)} %bitcast.5) | data formatting | bytes 524288

commit v4 on v3

--- a/solution.py
+++ b/solution.py
@@ -18,7 +18,7 @@
 ACROSS = 3.0
 FIRST_OWN = 3.0
 FAR_READY = 11.0
-PACE_DELAY = 0.0
+PACE_DELAY = 3.0
 PRODUCT_TIME = 2.7
 PIECES = 2
 

time: 78.8 us -> 78.6 us (level)
  no operation moved by 1% of the time
where the time goes in v4:
time: 78.6 us; the launch traced here: 77.6 us
  Pallas kernels  74.6 us (95%)
  local copies, waits for them, and re-layouts  1.67 us (2%)
  between operations  1.3 us (2%)
    pallas_call x1, Pallas kernels, per_device(): pl.pallas_call(kernel, out_shape=jax.ShapeDtypeStruct((vectors, share, co...  74.6 us
    unnamed x1, local copies, waits for them, and re-layouts  1.67 us

profile of v4, /device:TPU:1, one launch (start us, length us, event | category | flops | bytes accessed | tf_op | source)
XLA Modules:
  0.0 77.6 jit_solution(10278362780617498117)
XLA Ops:
  1.3 74.6 %shard_map.64 = bf16[8,64,256]{2,1,0:T(8,128)(2,1)} custom-call(s32[5]{0:T(128)} %shift_any.1, s32[1]{0:T(128)S(6)} %copy.8.left_dim, s32[1]{0:T(128)S(6)} %copy.9.right_dim, s32[5]{0:T(128)} %shift_any.1, bf16[8,64,256]{2,1,0:T(8,128)(2,1)} %bitcast.7, bf16[5,512,512]{2,1,0:T(8,128)(2,1)} %bitcast.4, bf16[5,256,256]{2,1,0:T(8,128)(2,1)} %bitcast.6), custom_call_target="tpu_custom_call" | custom-call | tf_op jit(solution)/shard_map/pallas_call | solution.py:334
  75.9 1.7 %copy.10 = bf16[1,8,64,256]{3,2,1,0:T(8,128)(2,1)} copy(bf16[1,8,64,256]{3,2,1,0:T(8,128)(2,1)} %bitcast.5) | data formatting | bytes 524288
